TPU v7x, 128 devices: a whole 4x4x4 slice. The times are simulated.
128 devices in a mesh: dp: 4 (over x), seq: 32 (over z, y, core).
Axes of the slice: x: 4, y: 4, z: 4, core: 2. Of those that a mesh axis runs over, the one named last changes fastest.
Arguments:
- conv_input: bfloat16 [16384, 5376], P(('dp', 'seq')), may hold values from -6 to 6
- doc_start: int32 [16384], P(('dp', 'seq')), may hold values 0 or 1
- conv_weight: float32 [4, 5376], replicated, may hold values from -3 to 3
- conv_bias: float32 [5376], replicated, may hold values from -0.5 to 0.5
- dt_raw: float32 [16384, 80], P(('dp', 'seq')), may hold values from -3 to 3
- dt_bias: float32 [80], replicated, may hold values from -5.5 to -4.2
- a_log: float32 [80], replicated, may hold values from -9 to 2, as said below
- skip_gain: float32 [80], replicated, may hold values from 0.5 to 1.5
- cotangent: bfloat16 [16384, 5120], P(('dp', 'seq')), may hold values from -6 to 6
Outputs:
- ssm_output: bfloat16 [16384, 5120], P(('dp', 'seq'))
- grad_input: bfloat16 [16384, 5376], P(('dp', 'seq'))
- grad_conv_weight: float32 [4, 5376], replicated
- grad_conv_bias: float32 [5376], replicated
- grad_dt_bias: float32 [80], replicated
- grad_a_log: float32 [80], replicated
- grad_skip_gain: float32 [80], replicated
Inputs may be any that keep to these rules, and one draw needn't show every extreme that they name: `doc_start`: 1 marks the first token of a document; documents may cross shard boundaries. One value per head; exp(a_log) lies between 25 / 4096 and 4.2, so that the per-token decay rates exp(a_log) * steps_dt run from under 1 / 4096 to about 1.1.
All inputs are finite; a program needn't handle non-finite values.
Results may differ from a plain program's by a relative error of at most 0.00115.
Values may be sent and summed in bfloat16 or wider, within the bound.
A program may use at most 320 MiB of HBM per device.

v0:
```python
import jax
import jax.numpy as jnp
from jax import lax
from jax.sharding import PartitionSpec as P

HEADS = 80
HEAD_DIM = 64
STATE = 128
CONV = 4
BLOCK = 64
INNER = 5120
exact_mode = lax.Precision.HIGHEST


def from_behind(array, axis, by):
    size = lax.axis_size(axis)
    pairs = [(i, i + by) for i in range(size) if 0 <= i + by < size]
    return lax.ppermute(array, axis, pairs)


def prefix(array, axis, combine, identity, reverse):
    size, place = (lax.axis_size(axis), lax.axis_index(axis))
    everything = jax.tree.map(lambda part: lax.all_gather(part, axis), array)
    start = jax.tree.map(
        lambda part, zero: jnp.broadcast_to(jnp.asarray(zero, part.dtype), part.shape),
        array,
        identity,
    )

    def step(k, before):
        at = size - 1 - k if reverse else k
        reached = at > place if reverse else at < place
        new = combine(before, jax.tree.map(lambda part: part[at], everything))
        return jax.tree.map(lambda a, b: jnp.where(reached, a, b), new, before)

    return lax.fori_loop(0, size, step, start)


def prepare_inputs(
    tail_rows, conv_input, doc_start, conv_weight, conv_bias, dt_raw, dt_bias, a_log
):
    row_count = conv_input.shape[0]
    extended = jnp.concatenate([tail_rows, conv_input], axis=0)
    resets = doc_start.astype(jnp.float32)
    segment = jnp.cumsum(resets)
    padded = jnp.concatenate([jnp.zeros((CONV - 1,), jnp.float32), segment])
    convolved = conv_bias[None, :] + conv_weight[CONV - 1][None, :] * extended[CONV - 1 :]
    for offset in range(1, CONV):
        first_row = CONV - 1 - offset
        tap_valid = (padded[first_row : first_row + row_count] == segment).astype(jnp.float32)
        convolved = (
            convolved
            + conv_weight[first_row][None, :]
            * extended[first_row : first_row + row_count]
            * tap_valid[:, None]
        )
    activated = jax.nn.silu(convolved)
    values_x = activated[:, :INNER].reshape(row_count, HEADS, HEAD_DIM)
    keys_b = activated[:, INNER : INNER + STATE]
    reads_c = activated[:, INNER + STATE :]
    steps_dt = jax.nn.softplus(dt_raw + dt_bias[None, :])
    log_decay = -jnp.exp(a_log)[None, :] * steps_dt
    return (values_x, keys_b, reads_c, steps_dt, log_decay)


def scan_block(carry, block_data):
    carry_state, skip_gain = carry
    values_x, keys_b, reads_c, steps_dt, log_decay, resets = block_data
    length = values_x.shape[0]
    segment = jnp.cumsum(resets)
    running = jnp.cumsum(log_decay, axis=0)
    positions = jnp.arange(length)
    causal = (positions[:, None] >= positions[None, :]) & (segment[:, None] == segment[None, :])
    spread_log = running.T[:, :, None] - running.T[:, None, :]
    within = jnp.where(causal[None], jnp.exp(jnp.where(causal[None], spread_log, 0.0)), 0.0)
    scores = jnp.dot(reads_c, keys_b.T, precision=exact_mode)
    weights = within * scores[None] * steps_dt.T[:, None, :]
    output = jnp.einsum("hts,shp->thp", weights, values_x, precision=exact_mode)
    untouched = (segment == 0).astype(running.dtype)
    entry_weight = jnp.exp(running) * untouched[:, None]
    output = (
        output
        + jnp.einsum("tn,hpn->thp", reads_c, carry_state, precision=exact_mode)
        * entry_weight[:, :, None]
    )
    output = output + skip_gain[None, :, None] * values_x
    last_segment = (segment == segment[length - 1]).astype(running.dtype)
    leave_weight = (
        jnp.exp(running[length - 1][None, :] - running) * last_segment[:, None] * steps_dt
    )
    through = jnp.exp(running[length - 1]) * untouched[length - 1]
    added = jnp.einsum(
        "shp,sn->hpn", leave_weight[:, :, None] * values_x, keys_b, precision=exact_mode
    )
    carry_state = carry_state * through[:, None, None] + added
    return ((carry_state, skip_gain), output)


def chain_blocks(values_x, keys_b, reads_c, steps_dt, log_decay, resets, skip_gain, start_state):
    row_count = values_x.shape[0]
    block_count = row_count // BLOCK
    pieces = tuple(
        (
            member.reshape((block_count, BLOCK) + member.shape[1:])
            for member in (values_x, keys_b, reads_c, steps_dt, log_decay, resets)
        )
    )
    stepper = jax.checkpoint(scan_block)
    (final_state, _), outputs = lax.scan(stepper, (start_state, skip_gain), pieces)
    return (outputs.reshape(row_count, INNER), final_state)


def join_states(earlier, later):
    return (earlier[0] * later[0], later[0][:, None, None] * earlier[1] + later[1])


def on_device(
    conv_input, doc_start, conv_weight, conv_bias, dt_raw, dt_bias, a_log, skip_gain, cotangent
):
    row_count = conv_input.shape[0]
    resets = doc_start.astype(jnp.float32)
    after = jnp.concatenate([1.0 - resets[row_count - CONV + 2 :], jnp.ones((1,), jnp.float32)])
    keep_rows = jnp.flip(jnp.cumprod(jnp.flip(after)))
    tail_out = conv_input[row_count - CONV + 1 :] * keep_rows[:, None].astype(jnp.bfloat16)
    tail_in = from_behind(tail_out, "seq", 1)

    def prepare_local(tail_rows, rows_value, weight_value, bias_value, dtb_value, alog_value):
        return prepare_inputs(
            tail_rows,
            rows_value,
            doc_start,
            weight_value,
            bias_value,
            dt_raw,
            dtb_value,
            alog_value,
        )

    prepared, pull_prep = jax.vjp(
        prepare_local,
        tail_in.astype(jnp.float32),
        conv_input.astype(jnp.float32),
        conv_weight,
        conv_bias,
        dt_bias,
        a_log,
    )
    values_x, keys_b, reads_c, steps_dt, log_decay = prepared
    zero_state = jnp.zeros((HEADS, HEAD_DIM, STATE), jnp.float32)

    def local_chain(x_value, b_value, c_value, dt_value, decay_value, gain_value):
        return chain_blocks(
            x_value, b_value, c_value, dt_value, decay_value, resets, gain_value, zero_state
        )

    (local_out, local_state), pull_chain = jax.vjp(
        local_chain, values_x, keys_b, reads_c, steps_dt, log_decay, skip_gain
    )

    def entering(decay_value):
        running = jnp.cumsum(decay_value, axis=0)
        untouched = (jnp.cumsum(resets) == 0).astype(running.dtype)
        return (
            jnp.exp(running) * untouched[:, None],
            jnp.exp(running[row_count - 1]) * untouched[row_count - 1],
        )

    entry_weight, through = entering(log_decay)
    upstream = cotangent.astype(jnp.float32)
    upstream_heads = upstream.reshape(row_count, HEADS, HEAD_DIM)
    adjoint_local = jnp.einsum(
        "thp,tn->hpn", upstream_heads * entry_weight[:, :, None], reads_c, precision=exact_mode
    )
    identity = (jnp.ones((HEADS,), jnp.float32), jnp.zeros((HEADS, HEAD_DIM, STATE), jnp.float32))
    incoming = prefix((through, local_state), "seq", join_states, identity, False)[1]
    adjoint_end = prefix((through, adjoint_local), "seq", join_states, identity, True)[1]

    def carried(c_value, decay_value):
        weight_in, through_in = entering(decay_value)
        added = (
            jnp.einsum("tn,hpn->thp", c_value, incoming, precision=exact_mode)
            * weight_in[:, :, None]
        )
        return (added.reshape(row_count, INNER), through_in[:, None, None] * incoming)

    (carried_out, _), pull_carried = jax.vjp(carried, reads_c, log_decay)
    output = (local_out + carried_out).astype(jnp.bfloat16)
    grad_x, grad_b, grad_c, grad_dt, grad_decay, grad_gain = pull_chain((upstream, adjoint_end))
    grad_c_extra, grad_decay_extra = pull_carried((upstream, adjoint_end))
    grad_tail, grad_rows, grad_weight, grad_bias, grad_dtb, grad_alog = pull_prep(
        (grad_x, grad_b, grad_c + grad_c_extra, grad_dt, grad_decay + grad_decay_extra)
    )
    returned = from_behind(grad_tail, "seq", -1)
    grad_rows = jnp.concatenate(
        [
            grad_rows[: row_count - CONV + 1],
            grad_rows[row_count - CONV + 1 :] + returned * keep_rows[:, None],
        ],
        axis=0,
    )
    summed = lax.psum((grad_weight, grad_bias, grad_dtb, grad_alog, grad_gain), ("dp", "seq"))
    scale = float(lax.axis_size("dp") * lax.axis_size("seq") * row_count) ** (-0.5)
    return (
        output,
        grad_rows.astype(jnp.bfloat16),
        summed[0] * scale,
        summed[1] * scale,
        summed[2] * scale,
        summed[3] * scale,
        summed[4] * scale,
    )


def solution(mesh):
    return jax.shard_map(
        on_device,
        mesh=mesh,
        in_specs=(
            P(("dp", "seq"), None),
            P(("dp", "seq")),
            P(),
            P(),
            P(("dp", "seq"), None),
            P(),
            P(),
            P(),
            P(("dp", "seq"), None),
        ),
        out_specs=(P(("dp", "seq"), None), P(("dp", "seq"), None), P(), P(), P(), P(), P()),
        check_vma=False,
    )
```

profile of v0, /device:TPU:1, one launch (start us, length us, event | category | flops | bytes accessed | tf_op | source)
XLA Modules:
  0.0 1133.3 jit_solution(11397604116379961711)
XLA Ops:
  21.4 7.5 fusion.100
  36.5 69.3 %while.76 = (s32[]{:T(128)}, f32[80,64,128]{2,1,0:T(8,128)S(1)}, f32[2,64,80,64]{3,2,1,0:T(8,128)}, f32[2,80,64,128]{3,2,1,0:T(8,128)}, f32[2,80]{1,0:T(2,128)S(...) while((s32[]{:T(128)}, f32[80,64,128]{2,1,0:T(8,128)S(1)}, ...), condition=%wide.region_5.6_spmd.clone, body=%wide.region_2.5_spmd.clone.sunk | while | flops 1271495936 | bytes 43904780 | solution.py:109
  50.0 5.3 multiply_add_fusion.7
  55.8 8.7 fusion.194
  90.4 8.7 fusion.194
  114.3 21.7 %all-gather.2 = f32[32,1,80]{2,1,0:T(1,128)S(1)} all-gather(f32[1,1,80]{2,1,0:T(1,128)S(1)} %multiply_bitcast_fusion), channel_id=1, replica_groups=mesh['dp'=4,'seq'=32] {'seq'}, dimensions={0}, use_global_device_ids=true | all-gather | bytes 10560 | tf_op jit(solution)/shard_map/all_gather | solution.py:23
  136.0 218.2 %all-gather.6.cloned.1.call-done = f32[2560,64,128]{2,1,0:T(8,128)} async-done(((f32[80,64,128]{2,1,0:T(8,128)}), f32[2560,64,128]{2,1,0:T(8,128)}) %all-gather.6.cloned.1.call-update) | async-done | bytes 83886096 | tf_op jit(solution)/shard_map/all_gather | solution.py:23
  354.3 77.1 %while.77 = (s32[]{:T(128)}, f32[80,64,128]{2,1,0:T(8,128)S(1)}, s32[]{:T(128)}, f32[32,80]{1,0:T(8,128)S(1)}, f32[32,80,64,128]{3,2,1,0:T(8,128)}, /*index=5*/s32[]{:T(128)}, s32[]{:T(128)}) while((s32[]{:T(128)}, f32[80,64,128]{2,1,0:T(8,128)S(1)}, s32[]{:T(128)}, f32[32,80]{1,0:T(8,128)S(1)}, f32[32,80,64,128]{3,2,1,0:T(8,128)}, ...), condition=%wide.region_8.9_spmd.clone, body=%wide.region_7.8_spmd.clone.sunk | while | flops 2621444 | bytes 7865393 | solution.py:36
  431.3 8.7 multiply_reduce_fusion.10
  446.7 6.0 reshape.542
  452.7 8.1 copy.125
  460.8 6.5 copy.124
  467.3 5.4 reshape.512
  484.9 205.6 %all-gather.8.cloned.1.call-done = f32[2560,64,128]{2,1,0:T(8,128)} async-done(((f32[80,64,128]{2,1,0:T(8,128)}), f32[2560,64,128]{2,1,0:T(8,128)}) %all-gather.8.cloned.1.call-update) | async-done | bytes 83886096 | tf_op jit(solution)/shard_map/all_gather | solution.py:23
  690.5 77.1 %while.78 = (s32[]{:T(128)}, f32[80,64,128]{2,1,0:T(8,128)S(1)}, s32[]{:T(128)}, f32[32,80]{1,0:T(8,128)S(1)}, f32[32,80,64,128]{3,2,1,0:T(8,128)}, /*index=5*/s32[]{:T(128)}, s32[]{:T(128)}, s32[]{:T(128)}, s32[]{:T(128)}) while((s32[]{:T(128)}, f32[80,64,128]{2,1,0:T(8,128)S(1)}, s32[]{:T(128)}, f32[32,80]{1,0:T(8,128)S(1)}, ...), condition=%wide.region_10.11_spmd.clone, body=%wide.region_9.10_spmd.clone.sunk | while | flops 2621448 | bytes 7865455 | solution.py:36
  772.6 176.0 %while.79 = (s32[]{:T(128)}, f32[80,64,128]{2,1,0:T(8,128)}, f32[80]{0:T(128)S(1)}, f32[2,64,80,64]{2,1,3,0:T(8,128)}, f32[2,64,128]{2,1,0:T(8,128)S(1)}, /*inde...) while((s32[]{:T(128)}, f32[80,64,128]{2,1,0:T(8,128)}, ...), condition=%wide.region_24.25_spmd.clone, body=%wide.region_11.24_spmd.clone.sunk | while | flops 3052656640 | bytes 114250048 | solution.py:109
  788.9 8.2 fusion.220
  797.3 9.1 multiply_reduce_fusion.17
  811.5 9.6 multiply_reduce_fusion.16
  830.5 6.4 multiply_add_fusion.8
  836.9 6.5 fusion.219
  873.0 8.2 fusion.220
  881.4 9.1 multiply_reduce_fusion.17
  895.6 9.6 multiply_reduce_fusion.16
  914.8 6.4 multiply_add_fusion.8
  921.2 6.5 fusion.219
  948.6 6.1 copy.127
  954.8 5.5 reshape.518
  960.3 7.3 fusion.110
  967.7 5.5 multiply_reduce_fusion.9
  986.6 66.0 %all-reduce.15 = (f32[5376]{0:T(1024)S(1)}, f32[80]{0:T(128)S(1)}, f32[80]{0:T(128)S(1)}, f32[80]{0:T(128)S(1)}) all-reduce(f32[5376]{0:T(1024)S(1)} %get-tuple-element.978, f32[80]{0:T(128)S(1)} %get-tuple-element.981, f32[80]{0:T(128)S(1)} %negate_multiply_fusion, ...), channel_id=1, replica_groups=mesh['dp'=4,'seq'=32] {'dp','seq'}, use_global_device_ids=true, to_apply=%region_31.32 | all-reduce | flops 5616 | bytes 44928 | tf_op jit(solution)/shard_map/psum | solution.py:201
  1057.0 65.2 %all-reduce.18.cloned.1.call-done = f32[4,5376]{1,0:T(4,128)} async-done(((f32[4,5376]{1,0:T(4,128)}), f32[4,5376]{1,0:T(4,128)}) %all-reduce.18.cloned.1.call-update) | async-done | bytes 86032 | tf_op jit(solution)/shard_map/psum | solution.py:201
  (457 shorter events, 361.2 us)
Async XLA Ops:
  7.2 14.3 %copy-start.37 = (f32[5376]{0:T(1024)S(1)}, f32[5376]{0:T(1024)}, u32[]{:S(2)}) copy-start(f32[5376]{0:T(1024)} %param.20) | copy-start | bytes 64516
  7.2 347.1 %all-gather.6.cloned.1.call-start = ((), (), s32[]{:S(2)}) async-start(), calls=%async_computation.1 | async-start | bytes 86507520 | tf_op jit(solution)/shard_map/all_gather | solution.py:23
  8.4 7.2 copy-start.50
  9.4 12.0 %collective-permute-start = (bf16[3,5376]{1,0:T(4,128)(2,1)S(1)}, bf16[3,5376]{1,0:T(4,128)(2,1)S(1)}, u32[]{:S(2)}, u32[]{:S(2)}) collective-permute-start(bf16[3,5376]{1,0:T(4,128)(2,1)S(1)} %slice_multiply_fusion), channel_id=1, source_target_pairs={{0,1},{1,2},{2,3},{3,4},{4,5},{5,6},{6,7},{7,8},{8,9},{9,10},{10,1... | collective-permute-start | bytes 96776 | tf_op jit(solution)/shard_map/ppermute | solution.py:18
  14.9 14.0 %copy-start.26 = (f32[128,80]{1,0:T(8,128)}, f32[128,80]{1,0:T(8,128)S(1)}, u32[]{:S(2)}) copy-start(f32[128,80]{1,0:T(8,128)S(1)} %copy.111) | copy-start | bytes 122884
  16.1 12.8 %copy-start.39 = (f32[128]{0:T(128)}, f32[128]{0:T(128)S(1)}, u32[]{:S(2)}) copy-start(f32[128]{0:T(128)S(1)} %get-tuple-element.1103) | copy-start | bytes 1540
  16.1 12.8 %copy-start.41 = (f32[128]{0:T(128)}, f32[128]{0:T(128)S(1)}, u32[]{:S(2)}) copy-start(f32[128]{0:T(128)S(1)} %get-tuple-element.1104) | copy-start | bytes 1540
  16.1 12.9 %copy-start.43 = (f32[128]{0:T(128)}, f32[128]{0:T(128)S(1)}, u32[]{:S(2)}) copy-start(f32[128]{0:T(128)S(1)} %get-tuple-element.1105) | copy-start | bytes 1540
  16.1 97.4 %copy-start.45 = (f32[128]{0:T(128)}, f32[128]{0:T(128)S(1)}, u32[]{:S(2)}) copy-start(f32[128]{0:T(128)S(1)} %get-tuple-element.1102) | copy-start | bytes 1540
  18.1 10.8 copy-start.29
  18.1 10.8 copy-start.31
  18.2 10.8 copy-start.33
  18.2 10.8 copy-start.35
  21.4 7.6 copy-start.22
  107.3 583.2 %all-gather.8.cloned.1.call-start = ((), (), s32[]{:S(2)}) async-start(), calls=%async_computation.2 | async-start | bytes 86507520 | tf_op jit(solution)/shard_map/all_gather | solution.py:23
  112.9 241.4 %copy-start.24 = (f32[128,80]{1,0:T(8,128)}, f32[128,80]{1,0:T(8,128)S(1)}, u32[]{:S(2)}) copy-start(f32[128,80]{1,0:T(8,128)S(1)} %reduce_window_sum.84) | copy-start | bytes 122884
  431.3 8.7 copy-start.5
  446.6 675.6 %all-reduce.18.cloned.1.call-start = ((), (), s32[]{:S(2)}) async-start(), calls=%async_computation | async-start | bytes 172032 | tf_op jit(solution)/shard_map/psum | solution.py:201
  797.3 9.1 copy-start
  830.5 6.4 copy-start.10
  881.3 9.1 copy-start
  914.8 6.4 copy-start.10
  954.8 12.9 %copy-start.23 = (f32[3,5376]{1,0:T(4,128)S(1)}, f32[3,5376]{1,0:T(4,128)}, u32[]{:S(2)}) copy-start(f32[3,5376]{1,0:T(4,128)} %copy-done.22) | copy-start | bytes 193540
  960.3 7.4 copy-start.17
  960.3 7.4 copy-start.20
  960.3 7.4 copy-start.40
  960.3 7.4 copy-start.42
  960.3 7.4 copy-start.44
  980.3 6.3 copy-start.52
  981.0 142.8 %copy-start.13 = (f32[128,5376]{1,0:T(8,128)S(1)}, f32[128,5376]{1,0:T(8,128)}, u32[]{:S(2)}) copy-start(f32[128,5376]{1,0:T(8,128)} %copy-done.12) | copy-start | bytes 8257540
  981.0 142.8 %copy-start.51 = (f32[3]{0:T(128)S(1)}, f32[3]{0:T(128)}, u32[]{:S(2)}) copy-start(f32[3]{0:T(128)} %copy-done.50) | copy-start | bytes 40
  981.0 142.8 %collective-permute-start.1 = (f32[3,5376]{1,0:T(4,128)S(1)}, f32[3,5376]{1,0:T(4,128)S(1)}, u32[]{:S(2)}, u32[]{:S(2)}) collective-permute-start(f32[3,5376]{1,0:T(4,128)S(1)} %pad_add_fusion.1), channel_id=1, source_target_pairs={{1,0},{2,1},{3,2},{4,3},{5,4},{6,5},{7,6},{8,7},{9,8},{10,9},{11,1... | collective-permute-start | bytes 193544 | tf_op jit(solution)/shard_map/ppermute | solution.py:18
  (33 other events, 133.0 us)
Sparse Core Ops, SparseCore 0:
  107.4 246.8 all-gather.5
  446.8 243.7 all-gather.7
  984.7 137.4 all-reduce.17
where the time goes:
time: 1140 us; the launch traced here: 1130 us
  waiting for transfers between devices  489 us (43%)
  other arithmetic  218 us (19%)
  matrix products  153 us (13%)
  local copies, waits for them, and re-layouts  151 us (13%)
  blocking collectives  87.7 us (8%)
  between operations  14.8 us (1%)
  loops' own time  12 us (1%)
    all_gather x2, waiting for transfers between devices, prefix(): everything = jax.tree.map(lambda part: lax.all_gather(part, axis), array)  424 us
    select_n x64, other arithmetic, step(): return jax.tree.map(lambda a, b: jnp.where(reached, a, b), new, before)  151 us
    psum x1, blocking collectives, on_device(): lax.psum((grad_weight, grad_bias, grad_dtb, grad_alog, grad_gain), ('dp',...  66 us
    psum x1, waiting for transfers between devices, on_device(): lax.psum((grad_weight, grad_bias, grad_dtb, grad_alog, grad_gain), ('dp',...  65.2 us
    dot_general x6, matrix products, scan_block(): output = jnp.einsum('hts,shp->thp', weights, values_x, precision=exact_mode)  46.7 us
    dot_general x8, matrix products, scan_block(): jnp.einsum('tn,hpn->thp', reads_c, carry_state, precision=exact_mode)  46.1 us
    dot_general x6, matrix products, scan_block(): jnp.einsum('shp,sn->hpn', leave_weight[:, :, None] * values_x, keys_b, pr...  37.8 us
    unnamed x97, local copies, waits for them, and re-layouts  28 us
  transfers between devices with their start and end apart: 5, of which 3 were waited for; matrix products, arithmetic and copies ran while one was open for 5% of the time, Pallas kernels for 0%

commit v1 on v0

--- a/solution.py
+++ b/solution.py
@@ -198,7 +198,9 @@
         ],
         axis=0,
     )
-    summed = lax.psum((grad_weight, grad_bias, grad_dtb, grad_alog, grad_gain), ("dp", "seq"))
+    summed = (grad_weight, grad_bias, grad_dtb, grad_alog, grad_gain)
+    for mesh_axis in ("seq", "dp"):
+        summed = lax.psum(summed, mesh_axis)
     scale = float(lax.axis_size("dp") * lax.axis_size("seq") * row_count) ** (-0.5)
     return (
         output,

time: 1140 us -> 1180 us (1.035)
  blocking collectives: 87.7 us -> 156 us
  waiting for transfers between devices: 489 us -> 463 us
    psum x1 -> x2, blocking collectives: 66 us -> 135 us  [on_device(): summed = lax.psum(summed, mesh_axis)]
    psum x1 -> x2, waiting for transfers between devices: 65.2 us -> 38.9 us  [on_device(): summed = lax.psum(summed, mesh_axis)]
  transfers between devices with their start and end apart: 5 -> 6, of which waited for: 3 -> 3; matrix products, arithmetic and copies ran while one was open for 5% -> 5% of each run, Pallas kernels for 0% -> 0%
where the time goes in v1:
time: 1180 us
  waiting for transfers between devices  463 us (39%)
  other arithmetic  218 us (18%)
  blocking collectives  156 us (13%)
  matrix products  153 us (13%)
  local copies, waits for them, and re-layouts  151 us (13%)
  between operations  14.8 us (1%)
  loops' own time  12.2 us (1%)
    all_gather x2, waiting for transfers between devices, prefix(): everything = jax.tree.map(lambda part: lax.all_gather(part, axis), array)  424 us
    select_n x64, other arithmetic, step(): return jax.tree.map(lambda a, b: jnp.where(reached, a, b), new, before)  151 us
    psum x2, blocking collectives, on_device(): summed = lax.psum(summed, mesh_axis)  135 us
    dot_general x6, matrix products, scan_block(): output = jnp.einsum('hts,shp->thp', weights, values_x, precision=exact_mode)  46.7 us
    dot_general x8, matrix products, scan_block(): jnp.einsum('tn,hpn->thp', reads_c, carry_state, precision=exact_mode)  46.1 us
    psum x2, waiting for transfers between devices, on_device(): summed = lax.psum(summed, mesh_axis)  38.9 us
    dot_general x6, matrix products, scan_block(): jnp.einsum('shp,sn->hpn', leave_weight[:, :, None] * values_x, keys_b, pr...  37.8 us
    unnamed x97, local copies, waits for them, and re-layouts  27.9 us
  transfers between devices with their start and end apart: 6, of which 3 were waited for; matrix products, arithmetic and copies ran while one was open for 5% of the time, Pallas kernels for 0%

profile of v1, /device:TPU:1, one launch (start us, length us, event | category | flops | bytes accessed | tf_op | source)
XLA Modules:
  0.0 1175.8 jit_solution(2728350878111553526)
XLA Ops:
  21.4 7.5 fusion.100
  36.5 69.3 %while.76 = (s32[]{:T(128)}, f32[80,64,128]{2,1,0:T(8,128)S(1)}, f32[2,64,80,64]{3,2,1,0:T(8,128)}, f32[2,80,64,128]{3,2,1,0:T(8,128)}, f32[2,80]{1,0:T(2,128)S(...) while((s32[]{:T(128)}, f32[80,64,128]{2,1,0:T(8,128)S(1)}, ...), condition=%wide.region_5.6_spmd.clone, body=%wide.region_2.5_spmd.clone.sunk | while | flops 1271495936 | bytes 43904780 | solution.py:109
  55.8 8.7 fusion.194
  90.4 8.7 fusion.194
  114.3 21.7 %all-gather.2 = f32[32,1,80]{2,1,0:T(1,128)S(1)} all-gather(f32[1,1,80]{2,1,0:T(1,128)S(1)} %multiply_bitcast_fusion), channel_id=1, replica_groups=mesh['dp'=4,'seq'=32] {'seq'}, dimensions={0}, use_global_device_ids=true | all-gather | bytes 10560 | tf_op jit(solution)/shard_map/all_gather | solution.py:23
  136.0 218.2 %all-gather.6.cloned.1.call-done = f32[2560,64,128]{2,1,0:T(8,128)} async-done(((f32[80,64,128]{2,1,0:T(8,128)}), f32[2560,64,128]{2,1,0:T(8,128)}) %all-gather.6.cloned.1.call-update) | async-done | bytes 83886096 | tf_op jit(solution)/shard_map/all_gather | solution.py:23
  354.3 77.1 %while.77 = (s32[]{:T(128)}, f32[80,64,128]{2,1,0:T(8,128)S(1)}, s32[]{:T(128)}, f32[32,80]{1,0:T(8,128)S(1)}, f32[32,80,64,128]{3,2,1,0:T(8,128)}, /*index=5*/s32[]{:T(128)}, s32[]{:T(128)}) while((s32[]{:T(128)}, f32[80,64,128]{2,1,0:T(8,128)S(1)}, s32[]{:T(128)}, f32[32,80]{1,0:T(8,128)S(1)}, f32[32,80,64,128]{3,2,1,0:T(8,128)}, ...), condition=%wide.region_8.9_spmd.clone, body=%wide.region_7.8_spmd.clone.sunk | while | flops 2621444 | bytes 7865393 | solution.py:36
  431.3 8.7 multiply_reduce_fusion.10
  446.7 6.0 reshape.542
  452.7 8.1 copy.125
  460.8 6.5 copy.124
  467.3 5.4 reshape.512
  484.9 205.6 %all-gather.8.cloned.1.call-done = f32[2560,64,128]{2,1,0:T(8,128)} async-done(((f32[80,64,128]{2,1,0:T(8,128)}), f32[2560,64,128]{2,1,0:T(8,128)}) %all-gather.8.cloned.1.call-update) | async-done | bytes 83886096 | tf_op jit(solution)/shard_map/all_gather | solution.py:23
  690.5 77.1 %while.78 = (s32[]{:T(128)}, f32[80,64,128]{2,1,0:T(8,128)S(1)}, s32[]{:T(128)}, f32[32,80]{1,0:T(8,128)S(1)}, f32[32,80,64,128]{3,2,1,0:T(8,128)}, /*index=5*/s32[]{:T(128)}, s32[]{:T(128)}, s32[]{:T(128)}, s32[]{:T(128)}) while((s32[]{:T(128)}, f32[80,64,128]{2,1,0:T(8,128)S(1)}, s32[]{:T(128)}, f32[32,80]{1,0:T(8,128)S(1)}, ...), condition=%wide.region_10.11_spmd.clone, body=%wide.region_9.10_spmd.clone.sunk | while | flops 2621448 | bytes 7865455 | solution.py:36
  772.6 176.2 %while.79 = (s32[]{:T(128)}, f32[80,64,128]{2,1,0:T(8,128)}, f32[80]{0:T(128)S(1)}, f32[2,64,80,64]{2,1,3,0:T(8,128)}, f32[2,64,128]{2,1,0:T(8,128)S(1)}, /*inde...) while((s32[]{:T(128)}, f32[80,64,128]{2,1,0:T(8,128)}, ...), condition=%wide.region_24.25_spmd.clone, body=%wide.region_11.24_spmd.clone.sunk | while | flops 3052656640 | bytes 114250048 | solution.py:109
  788.9 8.2 fusion.220
  797.3 9.1 multiply_reduce_fusion.17
  811.5 9.6 multiply_reduce_fusion.16
  830.5 6.4 multiply_add_fusion.8
  836.9 6.5 fusion.219
  873.0 8.2 fusion.220
  881.4 9.1 multiply_reduce_fusion.17
  895.6 9.6 multiply_reduce_fusion.16
  914.8 6.4 multiply_add_fusion.8
  921.2 6.5 fusion.219
  948.8 6.1 copy.127
  954.9 5.5 reshape.518
  960.4 7.3 fusion.110
  967.9 5.5 multiply_reduce_fusion.9
  986.8 121.2 %all-reduce.15 = (f32[5376]{0:T(1024)S(1)}, f32[80]{0:T(128)S(1)}, f32[80]{0:T(128)S(1)}, f32[80]{0:T(128)S(1)}) all-reduce(f32[5376]{0:T(1024)S(1)} %get-tuple-element.978, f32[80]{0:T(128)S(1)} %get-tuple-element.981, f32[80]{0:T(128)S(1)} %negate_multiply_fusion, ...), channel_id=1, replica_groups=mesh['dp'=4,'seq'=32] {'seq'}, use_global_device_ids=true, to_apply=%region_32.33 | all-reduce | flops 5616 | bytes 44928 | tf_op jit(solution)/shard_map/psum | solution.py:203
  1108.0 13.4 %all-reduce.16 = (f32[5376]{0:T(1024)S(1)}, f32[80]{0:T(128)S(1)}, f32[80]{0:T(128)S(1)}, f32[80]{0:T(128)S(1)}) all-reduce(f32[5376]{0:T(1024)S(1)} %get-tuple-element.1064, f32[80]{0:T(128)S(1)} %get-tuple-element.1065, f32[80]{0:T(128)S(1)} %get-tuple-element.1066, ...), channel_id=1, replica_groups=mesh['dp'=4,'seq'=32] {'dp'}, use_global_device_ids=true, to_apply=%region_33.34 | all-reduce | flops 5616 | bytes 44928 | tf_op jit(solution)/shard_map/psum | solution.py:203
  1128.6 38.9 %all-reduce.22.cloned.1.call-done = f32[4,5376]{1,0:T(4,128)} async-done(((f32[4,5376]{1,0:T(4,128)}), f32[4,5376]{1,0:T(4,128)}) %all-reduce.22.cloned.1.call-update) | async-done | bytes 86032 | tf_op jit(solution)/shard_map/psum | solution.py:203
  (461 shorter events, 366.5 us)
Async XLA Ops:
  7.2 14.3 %copy-start.37 = (f32[5376]{0:T(1024)S(1)}, f32[5376]{0:T(1024)}, u32[]{:S(2)}) copy-start(f32[5376]{0:T(1024)} %param.20) | copy-start | bytes 64516
  7.2 347.1 %all-gather.6.cloned.1.call-start = ((), (), s32[]{:S(2)}) async-start(), calls=%async_computation.2 | async-start | bytes 86507520 | tf_op jit(solution)/shard_map/all_gather | solution.py:23
  8.4 7.2 copy-start.50
  9.4 12.0 %collective-permute-start = (bf16[3,5376]{1,0:T(4,128)(2,1)S(1)}, bf16[3,5376]{1,0:T(4,128)(2,1)S(1)}, u32[]{:S(2)}, u32[]{:S(2)}) collective-permute-start(bf16[3,5376]{1,0:T(4,128)(2,1)S(1)} %slice_multiply_fusion), channel_id=1, source_target_pairs={{0,1},{1,2},{2,3},{3,4},{4,5},{5,6},{6,7},{7,8},{8,9},{9,10},{10,1... | collective-permute-start | bytes 96776 | tf_op jit(solution)/shard_map/ppermute | solution.py:18
  14.9 14.0 %copy-start.26 = (f32[128,80]{1,0:T(8,128)}, f32[128,80]{1,0:T(8,128)S(1)}, u32[]{:S(2)}) copy-start(f32[128,80]{1,0:T(8,128)S(1)} %copy.111) | copy-start | bytes 122884
  16.1 12.8 %copy-start.39 = (f32[128]{0:T(128)}, f32[128]{0:T(128)S(1)}, u32[]{:S(2)}) copy-start(f32[128]{0:T(128)S(1)} %get-tuple-element.1107) | copy-start | bytes 1540
  16.1 12.8 %copy-start.41 = (f32[128]{0:T(128)}, f32[128]{0:T(128)S(1)}, u32[]{:S(2)}) copy-start(f32[128]{0:T(128)S(1)} %get-tuple-element.1108) | copy-start | bytes 1540
  16.1 12.9 %copy-start.43 = (f32[128]{0:T(128)}, f32[128]{0:T(128)S(1)}, u32[]{:S(2)}) copy-start(f32[128]{0:T(128)S(1)} %get-tuple-element.1109) | copy-start | bytes 1540
  16.1 97.4 %copy-start.45 = (f32[128]{0:T(128)}, f32[128]{0:T(128)S(1)}, u32[]{:S(2)}) copy-start(f32[128]{0:T(128)S(1)} %get-tuple-element.1106) | copy-start | bytes 1540
  18.1 10.8 copy-start.29
  18.1 10.8 copy-start.31
  18.2 10.8 copy-start.33
  18.2 10.8 copy-start.35
  21.4 7.6 copy-start.22
  107.3 583.2 %all-gather.8.cloned.1.call-start = ((), (), s32[]{:S(2)}) async-start(), calls=%async_computation.3 | async-start | bytes 86507520 | tf_op jit(solution)/shard_map/all_gather | solution.py:23
  112.9 241.4 %copy-start.24 = (f32[128,80]{1,0:T(8,128)}, f32[128,80]{1,0:T(8,128)S(1)}, u32[]{:S(2)}) copy-start(f32[128,80]{1,0:T(8,128)S(1)} %reduce_window_sum.84) | copy-start | bytes 122884
  431.3 8.7 copy-start.5
  446.6 679.1 %all-reduce.20.cloned.1.call-start = ((), (), s32[]{:S(2)}) async-start(), calls=%async_computation | async-start | bytes 172032 | tf_op jit(solution)/shard_map/psum | solution.py:203
  797.3 9.1 copy-start
  830.5 6.4 copy-start.10
  881.3 9.1 copy-start
  914.8 6.4 copy-start.10
  954.9 12.9 %copy-start.23 = (f32[3,5376]{1,0:T(4,128)S(1)}, f32[3,5376]{1,0:T(4,128)}, u32[]{:S(2)}) copy-start(f32[3,5376]{1,0:T(4,128)} %copy-done.22) | copy-start | bytes 193540
  960.4 7.4 copy-start.17
  960.4 7.4 copy-start.20
  960.4 7.4 copy-start.40
  960.4 7.4 copy-start.42
  960.4 7.4 copy-start.44
  981.1 144.7 %copy-start.13 = (f32[128,5376]{1,0:T(8,128)S(1)}, f32[128,5376]{1,0:T(8,128)}, u32[]{:S(2)}) copy-start(f32[128,5376]{1,0:T(8,128)} %copy-done.12) | copy-start | bytes 8257540
  981.1 144.7 %copy-start.51 = (f32[3]{0:T(128)S(1)}, f32[3]{0:T(128)}, u32[]{:S(2)}) copy-start(f32[3]{0:T(128)} %copy-done.50) | copy-start | bytes 40
  981.1 144.7 %collective-permute-start.1 = (f32[3,5376]{1,0:T(4,128)S(1)}, f32[3,5376]{1,0:T(4,128)S(1)}, u32[]{:S(2)}, u32[]{:S(2)}) collective-permute-start(f32[3,5376]{1,0:T(4,128)S(1)} %pad_add_fusion.1), channel_id=1, source_target_pairs={{1,0},{2,1},{3,2},{4,3},{5,4},{6,5},{7,6},{8,7},{9,8},{10,9},{11,1... | collective-permute-start | bytes 193544 | tf_op jit(solution)/shard_map/ppermute | solution.py:18
  984.4 183.0 %all-reduce.22.cloned.1.call-start = ((), (), s32[]{:S(2)}) async-start(), calls=%async_computation.1 | async-start | bytes 172032 | tf_op jit(solution)/shard_map/psum | solution.py:203
  (34 other events, 139.6 us)
Sparse Core Ops, SparseCore 0:
  107.4 246.8 all-gather.5
  446.8 243.7 all-gather.7
  984.5 96.2 all-reduce.19
  1125.9 41.4 all-reduce.21
